TPU v7x, 512 devices: a whole 4x8x8 slice. The times are simulated.
512 devices in a mesh: chain: 64 (over y, x, core), cols: 8 (over z).
Axes of the slice: x: 4, y: 8, z: 8, core: 2. Of those that a mesh axis runs over, the one named last changes fastest.
Arguments:
- start_vectors: float32 [1024, 256, 256], P('chain', 'cols'), may hold values from -6 to 6
- factors: float32 [1024, 256, 256], P('chain', 'cols'), may hold values from -1.2 to 1.2, as said below
Outputs:
- vectors: float32 [1024, 256, 256], P('chain', 'cols')
- log_growth: float32 [256], P('cols')
Inputs may be any that keep to these rules, and one draw needn't show every extreme that they name: `factors`: the factor blocks of the shifted operator; every product of consecutive factor blocks is bounded.
All inputs are finite; a program needn't handle non-finite values.
Results may differ from a plain program's by a relative error of at most 0.0003.
Values sent between devices are 32-bit elements; how exact they have to be, the bound alone decides.
No kernel may reach another device: no remote copies, remote signals or barrier semaphores. Data moves between devices by JAX's collectives and lax.ppermute only.
A program may use at most 128 MiB of HBM per device.

v0:
```python
import jax
import jax.numpy as jnp
from jax import lax
from jax.sharding import PartitionSpec as P

eps_value = 1e-06


def from_behind(block, axis, distance):
    devices = range(lax.axis_size(axis))
    route = [(i - distance, i) for i in devices if i - distance in devices]
    return lax.ppermute(block, axis, route)


def transform(matrix, vectors_in):
    return lax.dot_general(
        vectors_in,
        matrix,
        (((1,), (1,)), ((), ())),
        precision=lax.Precision.HIGHEST,
        preferred_element_type=jnp.float32,
    )


def compose(later, earlier):
    return jnp.dot(
        later, earlier, precision=lax.Precision.HIGHEST, preferred_element_type=jnp.float32
    )


def forward_rows(factors, right_side, incoming):

    def forward_advance(carried, element):
        matrix, source = element
        carried = transform(matrix, carried) + source
        return (carried, carried)

    return lax.scan(forward_advance, incoming, (factors, right_side))


def backward_rows(factors, forward, incoming):

    def backward_advance(carried, element):
        matrix, source = element
        carried = transform(matrix, source + carried)
        return (carried, carried)

    return lax.scan(backward_advance, incoming, (factors, forward), reverse=True)


def chain_operator(factors, reverse):
    identity_block = jnp.eye(factors.shape[1], dtype=jnp.float32)

    def chain_advance(running, matrix):
        return (compose(matrix, running), None)

    running, _ = lax.scan(chain_advance, identity_block, factors, reverse=reverse)
    return running


def section_count():
    return (lax.axis_size("chain") - 1).bit_length()


def enter_state(summary, direction):
    return from_behind(summary, "chain", direction)


def solve_system(factors, right_side, prefix_forward, prefix_backward):
    zero_state = jnp.zeros(right_side.shape[1:], jnp.float32)
    local_last, _ = forward_rows(factors, right_side, zero_state)
    incoming = enter_state(prefix_forward(local_last), 1)
    _, forward = forward_rows(factors, right_side, incoming)
    local_first, _ = backward_rows(factors, forward, zero_state)
    incoming_back = enter_state(prefix_backward(local_first), -1)
    _, solved = backward_rows(factors, forward, incoming_back)
    return solved


def shards(start_vectors, factors):
    full_factors = lax.all_gather(factors, "cols", axis=1, tiled=True)

    def pair_prefix(operator, summary, direction):
        sections = section_count()
        for section_index in range(sections):
            distance = direction * (1 << section_index)
            if section_index + 1 < sections:
                received_op, received_sum = from_behind((operator, summary), "chain", distance)
                summary = transform(operator, received_sum) + summary
                operator = compose(operator, received_op)
            else:
                received_sum = from_behind(summary, "chain", distance)
                summary = transform(operator, received_sum) + summary
        return summary

    def prefix_forward(summary):
        return pair_prefix(chain_operator(full_factors, False), summary, 1)

    def prefix_backward(summary):
        return pair_prefix(chain_operator(full_factors, True), summary, -1)

    cell_count = start_vectors.shape[0] * lax.axis_size("chain") * start_vectors.shape[2]
    first_solve = solve_system(full_factors, start_vectors, prefix_forward, prefix_backward)
    first_squares = lax.psum(jnp.sum(first_solve * first_solve, axis=(0, 2)), "chain")
    scale_one = jnp.sqrt(first_squares / cell_count + eps_value)
    second_solve = solve_system(
        full_factors, first_solve / scale_one[None, :, None], prefix_forward, prefix_backward
    )
    second_squares = lax.psum(jnp.sum(second_solve * second_solve, axis=(0, 2)), "chain")
    scale_two = jnp.sqrt(second_squares / cell_count + eps_value)
    result_vectors = second_solve / scale_two[None, :, None]
    return (result_vectors, jnp.log(scale_two))


def solution(mesh):
    return jax.shard_map(
        shards,
        mesh=mesh,
        in_specs=(P("chain", "cols", None), P("chain", "cols", None)),
        out_specs=(P("chain", "cols", None), P("cols")),
        check_vma=False,
    )
```

profile of v0, /device:TPU:32, one launch (start us, length us, event | category | flops | bytes accessed | tf_op | source)
XLA Modules:
  0.0 812.4 jit_solution(6026892274242298097)
XLA Ops:
  8.0 64.7 %all-gather.2.cloned.1.call-done = f32[16,256,256]{2,1,0:T(8,128)} async-done(((f32[16,32,256]{2,1,0:T(8,128)}), f32[16,256,256]{2,1,0:T(8,128)}) %all-gather.2.cloned.1.call-update) | async-done | bytes 4194320 | tf_op jit(solution)/shard_map/all_gather | solution.py:81
  72.7 21.4 %while.146 = (s32[]{:T(128)}, f32[32,256]{1,0:T(8,128)S(1)}, f32[16,256,256]{2,1,0:T(8,128)}, f32[16,32,256]{2,1,0:T(8,128)}, s32[]{:T(128)}, /*index=5*/s32[]{:T(128)}) while((s32[]{:T(128)}, f32[32,256]{1,0:T(8,128)S(1)}, f32[16,256,256]{2,1,0:T(8,128)}, f32[16,32,256]{2,1,0:T(8,128)}, s32[]{:T(128)}, /*index=5*/s32[]{:T(128)}) %tuple.241), condition=%wide.region_1.2_spmd.clone, body=%wide.region_0.1_spmd.clone.sunk | while | flops 25182212 | bytes 427087 | solution.py:38
  94.1 1.9 collective-permute-start
  96.0 22.1 %while.138 = (s32[]{:T(128)}, f32[256,256]{1,0:T(8,128)S(1)}, f32[16,256,256]{2,1,0:T(8,128)}, s32[]{:T(128)}) while((s32[]{:T(128)}, f32[256,256]{1,0:T(8,128)S(1)}, f32[16,256,256]{2,1,0:T(8,128)}, s32[]{:T(128)}) %tuple.273), condition=%wide.region_3.4_spmd, body=%wide.region_2.3_spmd.sunk | while | flops 201326592 | bytes 1311285 | solution.py:57
  118.1 3.5 collective-permute-start.2
  122.0 3.4 collective-permute-start.1
  125.4 3.8 collective-permute-done.2
  131.8 2.7 collective-permute-start.3
  134.6 7.3 collective-permute-done.4
  144.5 1.9 collective-permute-start.5
  146.4 10.8 %collective-permute-done.6 = f32[256,256]{1,0:T(8,128)S(1)} collective-permute-done((f32[256,256]{1,0:T(8,128)S(1)}, f32[256,256]{1,0:T(8,128)S(1)}, u32[]{:S(2)}, u32[]{:S(2)}) %collective-permute-start.6) | collective-permute-done | bytes 262176 | tf_op jit(solution)/shard_map/ppermute | solution.py:12
  161.9 7.5 collective-permute-done.8
  169.7 1.9 collective-permute-start.10
  173.3 7.5 collective-permute-done.10
  184.0 6.6 collective-permute-done.11
  190.7 21.4 %while.139 = (s32[]{:T(128)}, f32[32,256]{1,0:T(8,128)S(1)}, f32[16,32,256]{2,1,0:T(8,128)S(1)}, f32[16,256,256]{2,1,0:T(8,128)}, f32[16,32,256]{2,1,0:T(8,128)}, /*index=5*/s32[]{:T(128)}) while((s32[]{:T(128)}, f32[32,256]{1,0:T(8,128)S(1)}, f32[16,32,256]{2,1,0:T(8,128)S(1)}, f32[16,256,256]{2,1,0:T(8,128)}, f32[16,32,256]{2,1,0:T(8,128)}, ...), condition=%wide.region_5.6_spmd, body=%wide.region_4.5_spmd.sunk | while | flops 25174016 | bytes 459845 | solution.py:38
  212.1 21.3 %while.140 = (s32[]{:T(128)}, f32[32,256]{1,0:T(8,128)S(1)}, f32[16,32,256]{2,1,0:T(8,128)S(1)}, f32[16,256,256]{2,1,0:T(8,128)}, s32[]{:T(128)}, /*index=5*/s32[]{:T(128)}) while((s32[]{:T(128)}, f32[32,256]{1,0:T(8,128)S(1)}, f32[16,32,256]{2,1,0:T(8,128)S(1)}, f32[16,256,256]{2,1,0:T(8,128)}, s32[]{:T(128)}, /*index=5*/s32[]{:T(128)}) %tuple.275), condition=%wide.region_7.8_spmd, body=%wide.region_6.7_spmd.sunk | while | flops 25174020 | bytes 427089 | solution.py:48
  235.4 22.1 %while.141 = (s32[]{:T(128)}, f32[256,256]{1,0:T(8,128)S(1)}, f32[16,256,256]{2,1,0:T(8,128)}, s32[]{:T(128)}, s32[]{:T(128)}) while((s32[]{:T(128)}, f32[256,256]{1,0:T(8,128)S(1)}, f32[16,256,256]{2,1,0:T(8,128)}, s32[]{:T(128)}, s32[]{:T(128)}) %tuple.276), condition=%wide.region_9.10_spmd, body=%wide.region_8.9_spmd.sunk | while | flops 201326592 | bytes 1310797 | solution.py:57
  259.8 1.9 collective-permute-start.13
  261.8 1.9 collective-permute-done.14
  264.1 1.9 collective-permute-start.16
  266.9 4.4 collective-permute-start.15
  271.4 2.5 collective-permute-done.16
  278.5 7.5 collective-permute-done.18
  286.3 2.1 collective-permute-start.20
  290.7 6.7 collective-permute-done.20
  301.4 13.4 %collective-permute-done.22 = f32[256,256]{1,0:T(8,128)S(1)} collective-permute-done((f32[256,256]{1,0:T(8,128)S(1)}, f32[256,256]{1,0:T(8,128)S(1)}, u32[]{:S(2)}, u32[]{:S(2)}) %collective-permute-start.22) | collective-permute-done | bytes 262176 | tf_op jit(solution)/shard_map/ppermute | solution.py:12
  315.6 5.5 collective-permute-start.23
  322.7 21.6 %while.142 = (s32[]{:T(128)}, f32[32,256]{1,0:T(8,128)S(1)}, f32[16,32,256]{2,1,0:T(8,128)S(1)}, f32[16,32,256]{2,1,0:T(8,128)}, f32[16,256,256]{2,1,0:T(8,128)}, /*index=5*/s32[]{:T(128)}, s32[]{:T(128)}) while((s32[]{:T(128)}, f32[32,256]{1,0:T(8,128)S(1)}, f32[16,32,256]{2,1,0:T(8,128)S(1)}, f32[16,32,256]{2,1,0:T(8,128)}, ...), condition=%wide.region_11.12_spmd, body=%wide.region_10.11_spmd.sunk | while | flops 25174020 | bytes 460377 | solution.py:48
  344.5 129.1 %psum.14 = f32[32]{0:T(128)S(1)} all-reduce(f32[32]{0:T(128)S(1)} %multiply_reduce_fusion.1), channel_id=1, replica_groups=mesh['chain'=64,'cols'=8] {'chain'}, use_global_device_ids=true, to_apply=%region_13.14 | all-reduce | flops 32 | bytes 256 | tf_op jit(solution)/shard_map/psum | solution.py:104
  474.5 21.5 %while.147 = (s32[]{:T(128)}, f32[32,256]{1,0:T(8,128)S(1)}, f32[16,256,256]{2,1,0:T(8,128)}, f32[16,32,256]{2,1,0:T(8,128)}, s32[]{:T(128)}, /*index=5*/s32[]{:T(128)}) while((s32[]{:T(128)}, f32[32,256]{1,0:T(8,128)S(1)}, f32[16,256,256]{2,1,0:T(8,128)}, f32[16,32,256]{2,1,0:T(8,128)}, s32[]{:T(128)}, ...), condition=%wide.region_15.16_spmd.clone, body=%wide.region_14.15_spmd.clone.sunk | while | flops 25182212 | bytes 427087 | solution.py:38
  497.9 6.6 collective-permute-done.24
  506.8 7.2 collective-permute-done.25
  514.4 2.1 collective-permute-start.26
  516.4 7.5 collective-permute-done.26
  526.2 5.1 collective-permute-done.27
  533.6 6.0 collective-permute-done.28
  541.4 8.2 %collective-permute-done.29 = f32[32,256]{1,0:T(8,128)S(1)} collective-permute-done((f32[32,256]{1,0:T(8,128)S(1)}, f32[32,256]{1,0:T(8,128)S(1)}, u32[]{:S(2)}, u32[]{:S(2)}) %collective-permute-start.29) | collective-permute-done | bytes 32800 | tf_op jit(solution)/shard_map/ppermute | solution.py:12
  551.9 6.6 collective-permute-done.30
  558.6 21.4 %while.143 = (s32[]{:T(128)}, f32[32,256]{1,0:T(8,128)S(1)}, f32[16,32,256]{2,1,0:T(8,128)S(1)}, f32[16,256,256]{2,1,0:T(8,128)}, f32[16,32,256]{2,1,0:T(8,128)}, /*index=5*/s32[]{:T(128)}) while((s32[]{:T(128)}, f32[32,256]{1,0:T(8,128)S(1)}, f32[16,32,256]{2,1,0:T(8,128)S(1)}, f32[16,256,256]{2,1,0:T(8,128)}, f32[16,32,256]{2,1,0:T(8,128)}, ...), condition=%wide.region_17.18_spmd, body=%wide.region_16.17_spmd.sunk | while | flops 25174016 | bytes 459845 | solution.py:38
  580.0 21.3 %while.144 = (s32[]{:T(128)}, f32[32,256]{1,0:T(8,128)S(1)}, f32[16,32,256]{2,1,0:T(8,128)S(1)}, f32[16,256,256]{2,1,0:T(8,128)}, s32[]{:T(128)}, /*index=5*/s32[]{:T(128)}) while((s32[]{:T(128)}, f32[32,256]{1,0:T(8,128)S(1)}, f32[16,32,256]{2,1,0:T(8,128)S(1)}, f32[16,256,256]{2,1,0:T(8,128)}, s32[]{:T(128)}, /*index=5*/s32[]{:T(128)}) %tuple.280), condition=%wide.region_19.20_spmd, body=%wide.region_18.19_spmd.sunk | while | flops 25174020 | bytes 427089 | solution.py:48
  607.1 3.9 collective-permute-done.32
  613.3 5.4 collective-permute-done.33
  620.9 4.1 collective-permute-done.34
  627.3 4.8 collective-permute-done.35
  635.6 16.2 %collective-permute-start.37 = (f32[32,256]{1,0:T(8,128)S(1)}, f32[32,256]{1,0:T(8,128)S(1)}, u32[]{:S(2)}, u32[]{:S(2)}) collective-permute-start(f32[32,256]{1,0:T(8,128)S(1)} %convolution_add_fusion), channel_id=1, source_target_pairs={{8,0},{16,8},{24,16},{32,24},{40,32},{48,40},{56,48},{64,56},{72,6... | collective-permute-start | bytes 98312 | tf_op jit(solution)/shard_map/ppermute | solution.py:12
  653.5 21.3 %while.145 = (s32[]{:T(128)}, f32[32,256]{1,0:T(8,128)S(1)}, f32[16,32,256]{2,1,0:T(8,128)S(1)}, f32[16,32,256]{2,1,0:T(8,128)S(1)}, f32[16,256,256]{2,1,0:T(8,128)}, /*index=5*/s32[]{:T(128)}, s32[]{:T(128)}) while((s32[]{:T(128)}, f32[32,256]{1,0:T(8,128)S(1)}, f32[16,32,256]{2,1,0:T(8,128)S(1)}, f32[16,32,256]{2,1,0:T(8,128)S(1)}, ...), condition=%wide.region_21.22_spmd, body=%wide.region_20.21_spmd.sunk | while | flops 25174020 | bytes 460377 | solution.py:48
  675.0 129.1 %psum.15 = f32[32]{0:T(128)S(1)} all-reduce(f32[32]{0:T(128)S(1)} %multiply_reduce_fusion), channel_id=1, replica_groups=mesh['chain'=64,'cols'=8] {'chain'}, use_global_device_ids=true, to_apply=%region_23.24 | all-reduce | flops 32 | bytes 256 | tf_op jit(solution)/shard_map/psum | solution.py:109
  (419 shorter events, 279.4 us)
Async XLA Ops:
  7.2 65.5 %all-gather.2.cloned.1.call-start = ((), (), s32[]{:S(2)}) async-start(), calls=%async_computation | async-start | bytes 4718592 | tf_op jit(solution)/shard_map/all_gather | solution.py:81
  94.1 27.5 %collective-permute-start = (f32[32,256]{1,0:T(8,128)S(1)}, f32[32,256]{1,0:T(8,128)S(1)}, u32[]{:S(2)}, u32[]{:S(2)}) collective-permute-start(f32[32,256]{1,0:T(8,128)S(1)} %get-tuple-element.568), channel_id=1, source_target_pairs={{0,8},{8,16},{16,24},{24,32},{32,40},{40,48},{48,56},{56,64},{64,7... | collective-permute-start | bytes 98312 | tf_op jit(solution)/shard_map/ppermute | solution.py:12
  118.1 11.0 %collective-permute-start.2 = (f32[256,256]{1,0:T(8,128)S(1)}, f32[256,256]{1,0:T(8,128)S(1)}, u32[]{:S(2)}, u32[]{:S(2)}) collective-permute-start(f32[256,256]{1,0:T(8,128)S(1)} %get-tuple-element.569), channel_id=1, source_target_pairs={{0,8},{8,16},{16,24},{24,32},{32,40},{40,48},{48,56},{56,64},{64,7... | collective-permute-start | bytes 786440 | tf_op jit(solution)/shard_map/ppermute | solution.py:12
  122.0 9.5 %collective-permute-start.1 = (f32[32,256]{1,0:T(8,128)S(1)}, f32[32,256]{1,0:T(8,128)S(1)}, u32[]{:S(2)}, u32[]{:S(2)}) collective-permute-start(f32[32,256]{1,0:T(8,128)S(1)} %convolution_add_fusion.23), channel_id=1, source_target_pairs={{0,16},{8,24},{16,32},{24,40},{32,48},{40,56},{48,64},{56,72},{64,... | collective-permute-start | bytes 98312 | tf_op jit(solution)/shard_map/ppermute | solution.py:12
  129.5 12.3 %collective-permute-start.4 = (f32[256,256]{1,0:T(8,128)S(1)}, f32[256,256]{1,0:T(8,128)S(1)}, u32[]{:S(2)}, u32[]{:S(2)}) collective-permute-start(f32[256,256]{1,0:T(8,128)S(1)} %fusion.54), channel_id=1, source_target_pairs={{0,16},{8,24},{16,32},{24,40},{32,48},{40,56},{48,64},{56,72},{64,... | collective-permute-start | bytes 786440 | tf_op jit(solution)/shard_map/ppermute | solution.py:12
  131.8 12.3 %collective-permute-start.3 = (f32[32,256]{1,0:T(8,128)S(1)}, f32[32,256]{1,0:T(8,128)S(1)}, u32[]{:S(2)}, u32[]{:S(2)}) collective-permute-start(f32[32,256]{1,0:T(8,128)S(1)} %convolution_add_fusion.22), channel_id=1, source_target_pairs={{0,32},{8,40},{16,48},{24,56},{32,64},{40,72},{48,80},{56,88},{64,... | collective-permute-start | bytes 98312 | tf_op jit(solution)/shard_map/ppermute | solution.py:12
  142.2 15.0 %collective-permute-start.6 = (f32[256,256]{1,0:T(8,128)S(1)}, f32[256,256]{1,0:T(8,128)S(1)}, u32[]{:S(2)}, u32[]{:S(2)}) collective-permute-start(f32[256,256]{1,0:T(8,128)S(1)} %fusion.55), channel_id=1, source_target_pairs={{0,32},{8,40},{16,48},{24,56},{32,64},{40,72},{48,80},{56,88},{64,... | collective-permute-start | bytes 786440 | tf_op jit(solution)/shard_map/ppermute | solution.py:12
  144.5 15.1 %collective-permute-start.5 = (f32[32,256]{1,0:T(8,128)S(1)}, f32[32,256]{1,0:T(8,128)S(1)}, u32[]{:S(2)}, u32[]{:S(2)}) collective-permute-start(f32[32,256]{1,0:T(8,128)S(1)} %convolution_add_fusion.21), channel_id=1, source_target_pairs={{0,64},{8,72},{16,80},{24,88},{32,96},{40,104},{48,112},{56,120},{... | collective-permute-start | bytes 98312 | tf_op jit(solution)/shard_map/ppermute | solution.py:12
  157.6 11.7 %collective-permute-start.8 = (f32[256,256]{1,0:T(8,128)S(1)}, f32[256,256]{1,0:T(8,128)S(1)}, u32[]{:S(2)}, u32[]{:S(2)}) collective-permute-start(f32[256,256]{1,0:T(8,128)S(1)} %fusion.56), channel_id=1, source_target_pairs={{0,64},{8,72},{16,80},{24,88},{32,96},{40,104},{48,112},{56,120},{... | collective-permute-start | bytes 786440 | tf_op jit(solution)/shard_map/ppermute | solution.py:12
  159.9 11.7 %collective-permute-start.7 = (f32[32,256]{1,0:T(8,128)S(1)}, f32[32,256]{1,0:T(8,128)S(1)}, u32[]{:S(2)}, u32[]{:S(2)}) collective-permute-start(f32[32,256]{1,0:T(8,128)S(1)} %convolution_add_fusion.20), channel_id=1, source_target_pairs={{0,128},{8,136},{16,144},{24,152},{32,160},{40,168},{48,176},{56,1... | collective-permute-start | bytes 98312 | tf_op jit(solution)/shard_map/ppermute | solution.py:12
  169.7 11.1 %collective-permute-start.10 = (f32[256,256]{1,0:T(8,128)S(1)}, f32[256,256]{1,0:T(8,128)S(1)}, u32[]{:S(2)}, u32[]{:S(2)}) collective-permute-start(f32[256,256]{1,0:T(8,128)S(1)} %fusion.57), channel_id=1, source_target_pairs={{0,128},{8,136},{16,144},{24,152},{32,160},{40,168},{48,176},{56,1... | collective-permute-start | bytes 786440 | tf_op jit(solution)/shard_map/ppermute | solution.py:12
  172.0 9.7 %collective-permute-start.9 = (f32[32,256]{1,0:T(8,128)S(1)}, f32[32,256]{1,0:T(8,128)S(1)}, u32[]{:S(2)}, u32[]{:S(2)}) collective-permute-start(f32[32,256]{1,0:T(8,128)S(1)} %convolution_add_fusion.19), channel_id=1, source_target_pairs={{0,256},{8,264},{16,272},{24,280},{32,288},{40,296},{48,304},{56,3... | collective-permute-start | bytes 98312 | tf_op jit(solution)/shard_map/ppermute | solution.py:12
  182.1 8.6 %collective-permute-start.11 = (f32[32,256]{1,0:T(8,128)S(1)}, f32[32,256]{1,0:T(8,128)S(1)}, u32[]{:S(2)}, u32[]{:S(2)}) collective-permute-start(f32[32,256]{1,0:T(8,128)S(1)} %convolution_add_fusion.18), channel_id=1, source_target_pairs={{0,8},{8,16},{16,24},{24,32},{32,40},{40,48},{48,56},{56,64},{64,7... | collective-permute-start | bytes 98312 | tf_op jit(solution)/shard_map/ppermute | solution.py:12
  233.4 28.3 %copy-start.2 = (f32[16,32,256]{2,1,0:T(8,128)}, f32[16,32,256]{2,1,0:T(8,128)S(1)}, u32[]{:S(2)}) copy-start(f32[16,32,256]{2,1,0:T(8,128)S(1)} %get-tuple-element.1180) | copy-start | bytes 1572868
  233.5 26.0 %collective-permute-start.12 = (f32[32,256]{1,0:T(8,128)S(1)}, f32[32,256]{1,0:T(8,128)S(1)}, u32[]{:S(2)}, u32[]{:S(2)}) collective-permute-start(f32[32,256]{1,0:T(8,128)S(1)} %get-tuple-element.571), channel_id=1, source_target_pairs={{8,0},{16,8},{24,16},{32,24},{40,32},{48,40},{56,48},{64,56},{72,6... | collective-permute-start | bytes 98312 | tf_op jit(solution)/shard_map/ppermute | solution.py:12
  257.5 6.1 collective-permute-start.14
  259.8 6.8 collective-permute-start.13
  264.1 9.8 %collective-permute-start.16 = (f32[256,256]{1,0:T(8,128)S(1)}, f32[256,256]{1,0:T(8,128)S(1)}, u32[]{:S(2)}, u32[]{:S(2)}) collective-permute-start(f32[256,256]{1,0:T(8,128)S(1)} %fusion.59), channel_id=1, source_target_pairs={{16,0},{24,8},{32,16},{40,24},{48,32},{56,40},{64,48},{72,56},{80,... | collective-permute-start | bytes 786440 | tf_op jit(solution)/shard_map/ppermute | solution.py:12
  266.9 9.2 %collective-permute-start.15 = (f32[32,256]{1,0:T(8,128)S(1)}, f32[32,256]{1,0:T(8,128)S(1)}, u32[]{:S(2)}, u32[]{:S(2)}) collective-permute-start(f32[32,256]{1,0:T(8,128)S(1)} %convolution_add_fusion.16), channel_id=1, source_target_pairs={{32,0},{40,8},{48,16},{56,24},{64,32},{72,40},{80,48},{88,56},{96,... | collective-permute-start | bytes 98312 | tf_op jit(solution)/shard_map/ppermute | solution.py:12
  274.3 11.7 %collective-permute-start.18 = (f32[256,256]{1,0:T(8,128)S(1)}, f32[256,256]{1,0:T(8,128)S(1)}, u32[]{:S(2)}, u32[]{:S(2)}) collective-permute-start(f32[256,256]{1,0:T(8,128)S(1)} %fusion.60), channel_id=1, source_target_pairs={{32,0},{40,8},{48,16},{56,24},{64,32},{72,40},{80,48},{88,56},{96,... | collective-permute-start | bytes 786440 | tf_op jit(solution)/shard_map/ppermute | solution.py:12
  276.5 11.9 %collective-permute-start.17 = (f32[32,256]{1,0:T(8,128)S(1)}, f32[32,256]{1,0:T(8,128)S(1)}, u32[]{:S(2)}, u32[]{:S(2)}) collective-permute-start(f32[32,256]{1,0:T(8,128)S(1)} %convolution_add_fusion.15), channel_id=1, source_target_pairs={{64,0},{72,8},{80,16},{88,24},{96,32},{104,40},{112,48},{120,56},{... | collective-permute-start | bytes 98312 | tf_op jit(solution)/shard_map/ppermute | solution.py:12
  286.3 11.1 %collective-permute-start.20 = (f32[256,256]{1,0:T(8,128)S(1)}, f32[256,256]{1,0:T(8,128)S(1)}, u32[]{:S(2)}, u32[]{:S(2)}) collective-permute-start(f32[256,256]{1,0:T(8,128)S(1)} %fusion.61), channel_id=1, source_target_pairs={{64,0},{72,8},{80,16},{88,24},{96,32},{104,40},{112,48},{120,56},{... | collective-permute-start | bytes 786440 | tf_op jit(solution)/shard_map/ppermute | solution.py:12
  288.8 11.0 %collective-permute-start.19 = (f32[32,256]{1,0:T(8,128)S(1)}, f32[32,256]{1,0:T(8,128)S(1)}, u32[]{:S(2)}, u32[]{:S(2)}) collective-permute-start(f32[32,256]{1,0:T(8,128)S(1)} %convolution_add_fusion.14), channel_id=1, source_target_pairs={{128,0},{136,8},{144,16},{152,24},{160,32},{168,40},{176,48},{184,... | collective-permute-start | bytes 98312 | tf_op jit(solution)/shard_map/ppermute | solution.py:12
  297.8 17.0 %collective-permute-start.22 = (f32[256,256]{1,0:T(8,128)S(1)}, f32[256,256]{1,0:T(8,128)S(1)}, u32[]{:S(2)}, u32[]{:S(2)}) collective-permute-start(f32[256,256]{1,0:T(8,128)S(1)} %fusion.62), channel_id=1, source_target_pairs={{128,0},{136,8},{144,16},{152,24},{160,32},{168,40},{176,48},{184,... | collective-permute-start | bytes 786440 | tf_op jit(solution)/shard_map/ppermute | solution.py:12
  300.1 15.1 %collective-permute-start.21 = (f32[32,256]{1,0:T(8,128)S(1)}, f32[32,256]{1,0:T(8,128)S(1)}, u32[]{:S(2)}, u32[]{:S(2)}) collective-permute-start(f32[32,256]{1,0:T(8,128)S(1)} %convolution_add_fusion.13), channel_id=1, source_target_pairs={{256,0},{264,8},{272,16},{280,24},{288,32},{296,40},{304,48},{312,... | collective-permute-start | bytes 98312 | tf_op jit(solution)/shard_map/ppermute | solution.py:12
  315.2 5.9 copy-start
  315.6 7.1 collective-permute-start.23
  496.0 8.6 %collective-permute-start.24 = (f32[32,256]{1,0:T(8,128)S(1)}, f32[32,256]{1,0:T(8,128)S(1)}, u32[]{:S(2)}, u32[]{:S(2)}) collective-permute-start(f32[32,256]{1,0:T(8,128)S(1)} %get-tuple-element.574), channel_id=1, source_target_pairs={{0,8},{8,16},{16,24},{24,32},{32,40},{40,48},{48,56},{56,64},{64,7... | collective-permute-start | bytes 98312 | tf_op jit(solution)/shard_map/ppermute | solution.py:12
  504.9 9.1 %collective-permute-start.25 = (f32[32,256]{1,0:T(8,128)S(1)}, f32[32,256]{1,0:T(8,128)S(1)}, u32[]{:S(2)}, u32[]{:S(2)}) collective-permute-start(f32[32,256]{1,0:T(8,128)S(1)} %convolution_add_fusion.11), channel_id=1, source_target_pairs={{0,16},{8,24},{16,32},{24,40},{32,48},{40,56},{48,64},{56,72},{64,... | collective-permute-start | bytes 98312 | tf_op jit(solution)/shard_map/ppermute | solution.py:12
  514.4 120.9 %copy-start.1 = (f32[256,256]{1,0:T(8,128)S(1)}, f32[256,256]{1,0:T(8,128)}, u32[]{:S(2)}) copy-start(f32[256,256]{1,0:T(8,128)} %copy-done) | copy-start | bytes 786436
  514.4 9.6 %collective-permute-start.26 = (f32[32,256]{1,0:T(8,128)S(1)}, f32[32,256]{1,0:T(8,128)S(1)}, u32[]{:S(2)}, u32[]{:S(2)}) collective-permute-start(f32[32,256]{1,0:T(8,128)S(1)} %convolution_add_fusion.10), channel_id=1, source_target_pairs={{0,32},{8,40},{16,48},{24,56},{32,64},{40,72},{48,80},{56,88},{64,... | collective-permute-start | bytes 98312 | tf_op jit(solution)/shard_map/ppermute | solution.py:12
  524.3 7.0 collective-permute-start.27
  531.6 7.9 collective-permute-start.28
  539.9 9.7 %collective-permute-start.29 = (f32[32,256]{1,0:T(8,128)S(1)}, f32[32,256]{1,0:T(8,128)S(1)}, u32[]{:S(2)}, u32[]{:S(2)}) collective-permute-start(f32[32,256]{1,0:T(8,128)S(1)} %convolution_add_fusion.7), channel_id=1, source_target_pairs={{0,256},{8,264},{16,272},{24,280},{32,288},{40,296},{48,304},{56,3... | collective-permute-start | bytes 98312 | tf_op jit(solution)/shard_map/ppermute | solution.py:12
  550.0 8.6 %collective-permute-start.30 = (f32[32,256]{1,0:T(8,128)S(1)}, f32[32,256]{1,0:T(8,128)S(1)}, u32[]{:S(2)}, u32[]{:S(2)}) collective-permute-start(f32[32,256]{1,0:T(8,128)S(1)} %convolution_add_fusion.6), channel_id=1, source_target_pairs={{0,8},{8,16},{16,24},{24,32},{32,40},{40,48},{48,56},{56,64},{64,7... | collective-permute-start | bytes 98312 | tf_op jit(solution)/shard_map/ppermute | solution.py:12
  601.3 3.5 collective-permute-start.31
  605.2 5.8 collective-permute-start.32
  611.3 7.3 collective-permute-start.33
  619.0 6.0 collective-permute-start.34
  625.3 6.7 collective-permute-start.35
  632.4 2.9 collective-permute-start.36
  635.6 17.8 %collective-permute-start.37 = (f32[32,256]{1,0:T(8,128)S(1)}, f32[32,256]{1,0:T(8,128)S(1)}, u32[]{:S(2)}, u32[]{:S(2)}) collective-permute-start(f32[32,256]{1,0:T(8,128)S(1)} %convolution_add_fusion), channel_id=1, source_target_pairs={{8,0},{16,8},{24,16},{32,24},{40,32},{48,40},{56,48},{64,56},{72,6... | collective-permute-start | bytes 98312 | tf_op jit(solution)/shard_map/ppermute | solution.py:12
Sparse Core Ops, SparseCore 0:
  10.1 62.5 all-gather.1
where the time goes:
time: 818 us; the launch traced here: 812 us
  blocking collectives  258 us (32%)
  matrix products  221 us (27%)
  waiting for transfers between devices  214 us (26%)
  starting transfers between devices  95.2 us (12%)
  between operations  14.9 us (2%)
    dot_general x152, matrix products, transform(): lax.dot_general(vectors_in, matrix, (((1,), (1,)), ((), ())), precision=l...  175 us
    ppermute x38, waiting for transfers between devices, from_behind(): return lax.ppermute(block, axis, route)  148 us
    psum x1, blocking collectives, shards(): lax.psum(jnp.sum(second_solve * second_solve, axis=(0, 2)), 'chain')  129 us
    psum x1, blocking collectives, shards(): lax.psum(jnp.sum(first_solve * first_solve, axis=(0, 2)), 'chain')  129 us
    ppermute x38, starting transfers between devices, from_behind(): return lax.ppermute(block, axis, route)  95.2 us
    all_gather x1, waiting for transfers between devices, shards(): full_factors = lax.all_gather(factors, 'cols', axis=1, tiled=True)  64.7 us
    dot_general x42, matrix products, compose(): jnp.dot(later, earlier, precision=lax.Precision.HIGHEST, preferred_elemen...  46.4 us
  transfers between devices with their start and end apart: 39, of which 29 were waited for; matrix products, arithmetic and copies ran while one was open for 6% of the time, Pallas kernels for 0%

commit v1 on v0

--- a/solution.py
+++ b/solution.py
@@ -1,9 +1,21 @@
+import functools
 import jax
 import jax.numpy as jnp
 from jax import lax
 from jax.sharding import PartitionSpec as P
 
 eps_value = 1e-06
+
+
+def notes_test(page, dim_no):
+    piece_out = jnp.concatenate(
+        lax.all_to_all(jnp.stack([page for _ in range(lax.axis_size("cols"))], 0), "cols", 0, 0),
+        dim_no,
+    )
+    return piece_out
+
+
+draw_map = functools.partial(notes_test, dim_no=1)
 
 
 def from_behind(block, axis, distance):
@@ -78,7 +90,7 @@
 
 
 def shards(start_vectors, factors):
-    full_factors = lax.all_gather(factors, "cols", axis=1, tiled=True)
+    full_factors = draw_map(factors)
 
     def pair_prefix(operator, summary, direction):
         sections = section_count()

time: 818 us -> 851 us (1.040)
  waiting for transfers between devices: 214 us -> 244 us
  between operations: 14.9 us -> 1.48 us
  local copies, waits for them, and re-layouts: 1.35 us -> 10.3 us
    all_to_all x0 -> x1, waiting for transfers between devices: none -> 96.2 us  [notes_test(): lax.all_to_all(jnp.stack([page for _ in range(lax.axis_size('cols'))], 0)...]
    all_gather x1 -> x0, waiting for transfers between devices: 64.7 us -> none  [shards(): full_factors = lax.all_gather(factors, 'cols', axis=1, tiled=True)]
    all_to_all x0 -> x1, starting transfers between devices: none -> 10.3 us  [notes_test(): lax.all_to_all(jnp.stack([page for _ in range(lax.axis_size('cols'))], 0)...]
where the time goes in v1:
time: 851 us; the launch traced here: 846 us
  blocking collectives  258 us (30%)
  waiting for transfers between devices  244 us (29%)
  matrix products  221 us (26%)
  starting transfers between devices  102 us (12%)
  local copies, waits for them, and re-layouts  10.3 us (1%)
    dot_general x152, matrix products, transform(): lax.dot_general(vectors_in, matrix, (((1,), (1,)), ((), ())), precision=l...  175 us
    ppermute x38, waiting for transfers between devices, from_behind(): return lax.ppermute(block, axis, route)  148 us
    psum x1, blocking collectives, shards(): lax.psum(jnp.sum(first_solve * first_solve, axis=(0, 2)), 'chain')  129 us
    psum x1, blocking collectives, shards(): lax.psum(jnp.sum(second_solve * second_solve, axis=(0, 2)), 'chain')  129 us
    all_to_all x1, waiting for transfers between devices, notes_test(): lax.all_to_all(jnp.stack([page for _ in range(lax.axis_size('cols'))], 0)...  96.2 us
    ppermute x38, starting transfers between devices, from_behind(): return lax.ppermute(block, axis, route)  91.9 us
    dot_general x42, matrix products, compose(): jnp.dot(later, earlier, precision=lax.Precision.HIGHEST, preferred_elemen...  46.4 us
  transfers between devices with their start and end apart: 39, of which 29 were waited for; matrix products, arithmetic and copies ran while one was open for 6% of the time, Pallas kernels for 0%

profile of v1, /device:TPU:32, one launch (start us, length us, event | category | flops | bytes accessed | tf_op | source)
XLA Modules:
  0.0 845.5 jit_solution(10647235117614062608)
XLA Ops:
  0.6 3.5 stack.2
  4.2 10.3 %all-to-all-start = ((f32[8,16,32,256]{3,2,1,0:T(8,128)}), f32[8,16,32,256]{3,2,1,0:T(8,128)}, u32[]{:S(2)}, u32[]{:S(2)}) async-start(f32[8,16,32,256]{3,2,1,0:T(8,128)} %stack.2), calls=%async_computation | async-start | bytes 8388608 | tf_op jit(solution)/shard_map/all_to_all | solution.py:12
  14.5 96.2 %all-to-all-done = f32[8,16,32,256]{3,2,1,0:T(8,128)} async-done(((f32[8,16,32,256]{3,2,1,0:T(8,128)}), f32[8,16,32,256]{3,2,1,0:T(8,128)}, u32[]{:S(2)}, u32[]{:S(2)}) %all-to-all-start) | async-done | bytes 4194336 | tf_op jit(solution)/shard_map/all_to_all | solution.py:12
  110.7 4.7 copy.4
  115.5 21.4 %while.146 = (s32[]{:T(128)}, f32[32,256]{1,0:T(8,128)S(1)}, f32[16,256,256]{2,1,0:T(8,128)}, f32[16,32,256]{2,1,0:T(8,128)}, s32[]{:T(128)}, /*index=5*/s32[]{:T(128)}) while((s32[]{:T(128)}, f32[32,256]{1,0:T(8,128)S(1)}, f32[16,256,256]{2,1,0:T(8,128)}, f32[16,32,256]{2,1,0:T(8,128)}, s32[]{:T(128)}, /*index=5*/s32[]{:T(128)}) %tuple.271), condition=%wide.region_1.2_spmd.clone, body=%wide.region_0.1_spmd.clone.sunk | while | flops 25182212 | bytes 427087 | solution.py:50
  136.9 1.9 collective-permute-start
  138.8 22.1 %while.138 = (s32[]{:T(128)}, f32[256,256]{1,0:T(8,128)S(1)}, f32[16,256,256]{2,1,0:T(8,128)}, s32[]{:T(128)}) while((s32[]{:T(128)}, f32[256,256]{1,0:T(8,128)S(1)}, f32[16,256,256]{2,1,0:T(8,128)}, s32[]{:T(128)}) %tuple.272), condition=%wide.region_3.4_spmd, body=%wide.region_2.3_spmd.sunk | while | flops 201326592 | bytes 1311285 | solution.py:69
  160.9 3.5 collective-permute-start.2
  164.8 3.4 collective-permute-start.1
  168.2 3.7 collective-permute-done.2
  174.6 2.8 collective-permute-start.3
  177.4 7.2 collective-permute-done.4
  189.2 10.8 %collective-permute-done.6 = f32[256,256]{1,0:T(8,128)S(1)} collective-permute-done((f32[256,256]{1,0:T(8,128)S(1)}, f32[256,256]{1,0:T(8,128)S(1)}, u32[]{:S(2)}, u32[]{:S(2)}) %collective-permute-start.6) | collective-permute-done | bytes 262176 | tf_op jit(solution)/shard_map/ppermute | solution.py:24
  202.7 1.9 collective-permute-start.7
  204.6 7.4 collective-permute-done.8
  216.0 7.5 collective-permute-done.10
  226.7 6.6 collective-permute-done.11
  233.4 21.4 %while.139 = (s32[]{:T(128)}, f32[32,256]{1,0:T(8,128)S(1)}, f32[16,32,256]{2,1,0:T(8,128)S(1)}, f32[16,256,256]{2,1,0:T(8,128)}, f32[16,32,256]{2,1,0:T(8,128)}, /*index=5*/s32[]{:T(128)}) while((s32[]{:T(128)}, f32[32,256]{1,0:T(8,128)S(1)}, f32[16,32,256]{2,1,0:T(8,128)S(1)}, f32[16,256,256]{2,1,0:T(8,128)}, f32[16,32,256]{2,1,0:T(8,128)}, ...), condition=%wide.region_5.6_spmd, body=%wide.region_4.5_spmd.sunk | while | flops 25174016 | bytes 459845 | solution.py:50
  254.9 21.3 %while.140 = (s32[]{:T(128)}, f32[32,256]{1,0:T(8,128)S(1)}, f32[16,32,256]{2,1,0:T(8,128)S(1)}, f32[16,256,256]{2,1,0:T(8,128)}, s32[]{:T(128)}, /*index=5*/s32[]{:T(128)}) while((s32[]{:T(128)}, f32[32,256]{1,0:T(8,128)S(1)}, f32[16,32,256]{2,1,0:T(8,128)S(1)}, f32[16,256,256]{2,1,0:T(8,128)}, s32[]{:T(128)}, /*index=5*/s32[]{:T(128)}) %tuple.274), condition=%wide.region_7.8_spmd, body=%wide.region_6.7_spmd.sunk | while | flops 25174020 | bytes 427089 | solution.py:60
  276.2 1.9 collective-permute-start.12
  278.1 22.1 %while.141 = (s32[]{:T(128)}, f32[256,256]{1,0:T(8,128)S(1)}, f32[16,256,256]{2,1,0:T(8,128)}, s32[]{:T(128)}, s32[]{:T(128)}) while((s32[]{:T(128)}, f32[256,256]{1,0:T(8,128)S(1)}, f32[16,256,256]{2,1,0:T(8,128)}, s32[]{:T(128)}, s32[]{:T(128)}) %tuple.275), condition=%wide.region_9.10_spmd, body=%wide.region_8.9_spmd.sunk | while | flops 201326592 | bytes 1310797 | solution.py:69
  309.7 4.5 collective-permute-start.15
  314.2 2.4 collective-permute-done.16
  321.2 7.5 collective-permute-done.18
  329.0 2.2 collective-permute-start.20
  333.5 6.7 collective-permute-done.20
  344.2 13.5 %collective-permute-done.22 = f32[256,256]{1,0:T(8,128)S(1)} collective-permute-done((f32[256,256]{1,0:T(8,128)S(1)}, f32[256,256]{1,0:T(8,128)S(1)}, u32[]{:S(2)}, u32[]{:S(2)}) %collective-permute-start.22) | collective-permute-done | bytes 262176 | tf_op jit(solution)/shard_map/ppermute | solution.py:24
  362.7 21.6 %while.142 = (s32[]{:T(128)}, f32[32,256]{1,0:T(8,128)S(1)}, f32[16,32,256]{2,1,0:T(8,128)S(1)}, f32[16,32,256]{2,1,0:T(8,128)}, f32[16,256,256]{2,1,0:T(8,128)}, /*index=5*/s32[]{:T(128)}, s32[]{:T(128)}) while((s32[]{:T(128)}, f32[32,256]{1,0:T(8,128)S(1)}, f32[16,32,256]{2,1,0:T(8,128)S(1)}, f32[16,32,256]{2,1,0:T(8,128)}, ...), condition=%wide.region_11.12_spmd, body=%wide.region_10.11_spmd.sunk | while | flops 25174020 | bytes 460377 | solution.py:60
  384.5 129.1 %psum.14 = f32[32]{0:T(128)S(1)} all-reduce(f32[32]{0:T(128)S(1)} %multiply_reduce_fusion.1), channel_id=1, replica_groups=mesh['chain'=64,'cols'=8] {'chain'}, use_global_device_ids=true, to_apply=%region_13.14 | all-reduce | flops 32 | bytes 256 | tf_op jit(solution)/shard_map/psum | solution.py:116
  514.6 21.5 %while.147 = (s32[]{:T(128)}, f32[32,256]{1,0:T(8,128)S(1)}, f32[16,256,256]{2,1,0:T(8,128)}, f32[16,32,256]{2,1,0:T(8,128)}, s32[]{:T(128)}, /*index=5*/s32[]{:T(128)}) while((s32[]{:T(128)}, f32[32,256]{1,0:T(8,128)S(1)}, f32[16,256,256]{2,1,0:T(8,128)}, f32[16,32,256]{2,1,0:T(8,128)}, s32[]{:T(128)}, ...), condition=%wide.region_15.16_spmd.clone, body=%wide.region_14.15_spmd.clone.sunk | while | flops 25182212 | bytes 427087 | solution.py:50
  537.9 6.6 collective-permute-done.24
  546.8 7.2 collective-permute-done.25
  554.4 2.1 collective-permute-start.26
  556.5 7.5 collective-permute-done.26
  564.3 2.1 collective-permute-start.27
  566.4 4.9 collective-permute-done.27
  573.6 6.0 collective-permute-done.28
  581.2 8.4 collective-permute-done.29
  591.9 6.6 collective-permute-done.30
  598.6 21.4 %while.143 = (s32[]{:T(128)}, f32[32,256]{1,0:T(8,128)S(1)}, f32[16,32,256]{2,1,0:T(8,128)S(1)}, f32[16,256,256]{2,1,0:T(8,128)}, f32[16,32,256]{2,1,0:T(8,128)}, /*index=5*/s32[]{:T(128)}) while((s32[]{:T(128)}, f32[32,256]{1,0:T(8,128)S(1)}, f32[16,32,256]{2,1,0:T(8,128)S(1)}, f32[16,256,256]{2,1,0:T(8,128)}, f32[16,32,256]{2,1,0:T(8,128)}, ...), condition=%wide.region_17.18_spmd, body=%wide.region_16.17_spmd.sunk | while | flops 25174016 | bytes 459845 | solution.py:50
  620.0 21.3 %while.144 = (s32[]{:T(128)}, f32[32,256]{1,0:T(8,128)S(1)}, f32[16,32,256]{2,1,0:T(8,128)S(1)}, f32[16,256,256]{2,1,0:T(8,128)}, s32[]{:T(128)}, /*index=5*/s32[]{:T(128)}) while((s32[]{:T(128)}, f32[32,256]{1,0:T(8,128)S(1)}, f32[16,32,256]{2,1,0:T(8,128)S(1)}, f32[16,256,256]{2,1,0:T(8,128)}, s32[]{:T(128)}, /*index=5*/s32[]{:T(128)}) %tuple.279), condition=%wide.region_19.20_spmd, body=%wide.region_18.19_spmd.sunk | while | flops 25174020 | bytes 427089 | solution.py:60
  647.1 3.9 collective-permute-done.32
  653.3 5.4 collective-permute-done.33
  661.0 4.1 collective-permute-done.34
  667.3 4.8 collective-permute-done.35
  675.6 16.3 %collective-permute-start.37 = (f32[32,256]{1,0:T(8,128)S(1)}, f32[32,256]{1,0:T(8,128)S(1)}, u32[]{:S(2)}, u32[]{:S(2)}) collective-permute-start(f32[32,256]{1,0:T(8,128)S(1)} %convolution_add_fusion), channel_id=1, source_target_pairs={{8,0},{16,8},{24,16},{32,24},{40,32},{48,40},{56,48},{64,56},{72,6... | collective-permute-start | bytes 98312 | tf_op jit(solution)/shard_map/ppermute | solution.py:24
  693.5 21.3 %while.145 = (s32[]{:T(128)}, f32[32,256]{1,0:T(8,128)S(1)}, f32[16,32,256]{2,1,0:T(8,128)S(1)}, f32[16,32,256]{2,1,0:T(8,128)S(1)}, f32[16,256,256]{2,1,0:T(8,128)}, /*index=5*/s32[]{:T(128)}, s32[]{:T(128)}) while((s32[]{:T(128)}, f32[32,256]{1,0:T(8,128)S(1)}, f32[16,32,256]{2,1,0:T(8,128)S(1)}, f32[16,32,256]{2,1,0:T(8,128)S(1)}, ...), condition=%wide.region_21.22_spmd, body=%wide.region_20.21_spmd.sunk | while | flops 25174020 | bytes 460377 | solution.py:60
  715.0 129.1 %psum.15 = f32[32]{0:T(128)S(1)} all-reduce(f32[32]{0:T(128)S(1)} %multiply_reduce_fusion), channel_id=1, replica_groups=mesh['chain'=64,'cols'=8] {'chain'}, use_global_device_ids=true, to_apply=%region_23.24 | all-reduce | flops 32 | bytes 256 | tf_op jit(solution)/shard_map/psum | solution.py:121
  (420 shorter events, 285.0 us)
Async XLA Ops:
  4.2 106.6 %all-to-all-start = ((f32[8,16,32,256]{3,2,1,0:T(8,128)}), f32[8,16,32,256]{3,2,1,0:T(8,128)}, u32[]{:S(2)}, u32[]{:S(2)}) async-start(f32[8,16,32,256]{3,2,1,0:T(8,128)} %stack.2), calls=%async_computation | async-start | bytes 8388608 | tf_op jit(solution)/shard_map/all_to_all | solution.py:12
  136.9 27.5 %collective-permute-start = (f32[32,256]{1,0:T(8,128)S(1)}, f32[32,256]{1,0:T(8,128)S(1)}, u32[]{:S(2)}, u32[]{:S(2)}) collective-permute-start(f32[32,256]{1,0:T(8,128)S(1)} %get-tuple-element.568), channel_id=1, source_target_pairs={{0,8},{8,16},{16,24},{24,32},{32,40},{40,48},{48,56},{56,64},{64,7... | collective-permute-start | bytes 98312 | tf_op jit(solution)/shard_map/ppermute | solution.py:24
  160.9 11.0 %collective-permute-start.2 = (f32[256,256]{1,0:T(8,128)S(1)}, f32[256,256]{1,0:T(8,128)S(1)}, u32[]{:S(2)}, u32[]{:S(2)}) collective-permute-start(f32[256,256]{1,0:T(8,128)S(1)} %get-tuple-element.569), channel_id=1, source_target_pairs={{0,8},{8,16},{16,24},{24,32},{32,40},{40,48},{48,56},{56,64},{64,7... | collective-permute-start | bytes 786440 | tf_op jit(solution)/shard_map/ppermute | solution.py:24
  164.8 9.5 %collective-permute-start.1 = (f32[32,256]{1,0:T(8,128)S(1)}, f32[32,256]{1,0:T(8,128)S(1)}, u32[]{:S(2)}, u32[]{:S(2)}) collective-permute-start(f32[32,256]{1,0:T(8,128)S(1)} %convolution_add_fusion.23), channel_id=1, source_target_pairs={{0,16},{8,24},{16,32},{24,40},{32,48},{40,56},{48,64},{56,72},{64,... | collective-permute-start | bytes 98312 | tf_op jit(solution)/shard_map/ppermute | solution.py:24
  172.3 12.3 %collective-permute-start.4 = (f32[256,256]{1,0:T(8,128)S(1)}, f32[256,256]{1,0:T(8,128)S(1)}, u32[]{:S(2)}, u32[]{:S(2)}) collective-permute-start(f32[256,256]{1,0:T(8,128)S(1)} %fusion.54), channel_id=1, source_target_pairs={{0,16},{8,24},{16,32},{24,40},{32,48},{40,56},{48,64},{56,72},{64,... | collective-permute-start | bytes 786440 | tf_op jit(solution)/shard_map/ppermute | solution.py:24
  174.6 12.3 %collective-permute-start.3 = (f32[32,256]{1,0:T(8,128)S(1)}, f32[32,256]{1,0:T(8,128)S(1)}, u32[]{:S(2)}, u32[]{:S(2)}) collective-permute-start(f32[32,256]{1,0:T(8,128)S(1)} %convolution_add_fusion.22), channel_id=1, source_target_pairs={{0,32},{8,40},{16,48},{24,56},{32,64},{40,72},{48,80},{56,88},{64,... | collective-permute-start | bytes 98312 | tf_op jit(solution)/shard_map/ppermute | solution.py:24
  185.0 15.0 %collective-permute-start.6 = (f32[256,256]{1,0:T(8,128)S(1)}, f32[256,256]{1,0:T(8,128)S(1)}, u32[]{:S(2)}, u32[]{:S(2)}) collective-permute-start(f32[256,256]{1,0:T(8,128)S(1)} %fusion.55), channel_id=1, source_target_pairs={{0,32},{8,40},{16,48},{24,56},{32,64},{40,72},{48,80},{56,88},{64,... | collective-permute-start | bytes 786440 | tf_op jit(solution)/shard_map/ppermute | solution.py:24
  187.3 15.1 %collective-permute-start.5 = (f32[32,256]{1,0:T(8,128)S(1)}, f32[32,256]{1,0:T(8,128)S(1)}, u32[]{:S(2)}, u32[]{:S(2)}) collective-permute-start(f32[32,256]{1,0:T(8,128)S(1)} %convolution_add_fusion.21), channel_id=1, source_target_pairs={{0,64},{8,72},{16,80},{24,88},{32,96},{40,104},{48,112},{56,120},{... | collective-permute-start | bytes 98312 | tf_op jit(solution)/shard_map/ppermute | solution.py:24
  200.4 11.6 %collective-permute-start.8 = (f32[256,256]{1,0:T(8,128)S(1)}, f32[256,256]{1,0:T(8,128)S(1)}, u32[]{:S(2)}, u32[]{:S(2)}) collective-permute-start(f32[256,256]{1,0:T(8,128)S(1)} %fusion.56), channel_id=1, source_target_pairs={{0,64},{8,72},{16,80},{24,88},{32,96},{40,104},{48,112},{56,120},{... | collective-permute-start | bytes 786440 | tf_op jit(solution)/shard_map/ppermute | solution.py:24
  202.7 11.7 %collective-permute-start.7 = (f32[32,256]{1,0:T(8,128)S(1)}, f32[32,256]{1,0:T(8,128)S(1)}, u32[]{:S(2)}, u32[]{:S(2)}) collective-permute-start(f32[32,256]{1,0:T(8,128)S(1)} %convolution_add_fusion.20), channel_id=1, source_target_pairs={{0,128},{8,136},{16,144},{24,152},{32,160},{40,168},{48,176},{56,1... | collective-permute-start | bytes 98312 | tf_op jit(solution)/shard_map/ppermute | solution.py:24
  212.4 11.0 %collective-permute-start.10 = (f32[256,256]{1,0:T(8,128)S(1)}, f32[256,256]{1,0:T(8,128)S(1)}, u32[]{:S(2)}, u32[]{:S(2)}) collective-permute-start(f32[256,256]{1,0:T(8,128)S(1)} %fusion.57), channel_id=1, source_target_pairs={{0,128},{8,136},{16,144},{24,152},{32,160},{40,168},{48,176},{56,1... | collective-permute-start | bytes 786440 | tf_op jit(solution)/shard_map/ppermute | solution.py:24
  214.7 9.7 %collective-permute-start.9 = (f32[32,256]{1,0:T(8,128)S(1)}, f32[32,256]{1,0:T(8,128)S(1)}, u32[]{:S(2)}, u32[]{:S(2)}) collective-permute-start(f32[32,256]{1,0:T(8,128)S(1)} %convolution_add_fusion.19), channel_id=1, source_target_pairs={{0,256},{8,264},{16,272},{24,280},{32,288},{40,296},{48,304},{56,3... | collective-permute-start | bytes 98312 | tf_op jit(solution)/shard_map/ppermute | solution.py:24
  224.8 8.6 %collective-permute-start.11 = (f32[32,256]{1,0:T(8,128)S(1)}, f32[32,256]{1,0:T(8,128)S(1)}, u32[]{:S(2)}, u32[]{:S(2)}) collective-permute-start(f32[32,256]{1,0:T(8,128)S(1)} %convolution_add_fusion.18), channel_id=1, source_target_pairs={{0,8},{8,16},{16,24},{24,32},{32,40},{40,48},{48,56},{56,64},{64,7... | collective-permute-start | bytes 98312 | tf_op jit(solution)/shard_map/ppermute | solution.py:24
  276.2 28.3 %copy-start.2 = (f32[16,32,256]{2,1,0:T(8,128)}, f32[16,32,256]{2,1,0:T(8,128)S(1)}, u32[]{:S(2)}) copy-start(f32[16,32,256]{2,1,0:T(8,128)S(1)} %get-tuple-element.1180) | copy-start | bytes 1572868
  276.2 26.0 %collective-permute-start.12 = (f32[32,256]{1,0:T(8,128)S(1)}, f32[32,256]{1,0:T(8,128)S(1)}, u32[]{:S(2)}, u32[]{:S(2)}) collective-permute-start(f32[32,256]{1,0:T(8,128)S(1)} %get-tuple-element.571), channel_id=1, source_target_pairs={{8,0},{16,8},{24,16},{32,24},{40,32},{48,40},{56,48},{64,56},{72,6... | collective-permute-start | bytes 98312 | tf_op jit(solution)/shard_map/ppermute | solution.py:24
  300.3 6.1 collective-permute-start.14
  302.5 6.8 collective-permute-start.13
  306.8 9.8 %collective-permute-start.16 = (f32[256,256]{1,0:T(8,128)S(1)}, f32[256,256]{1,0:T(8,128)S(1)}, u32[]{:S(2)}, u32[]{:S(2)}) collective-permute-start(f32[256,256]{1,0:T(8,128)S(1)} %fusion.59), channel_id=1, source_target_pairs={{16,0},{24,8},{32,16},{40,24},{48,32},{56,40},{64,48},{72,56},{80,... | collective-permute-start | bytes 786440 | tf_op jit(solution)/shard_map/ppermute | solution.py:24
  309.7 9.2 %collective-permute-start.15 = (f32[32,256]{1,0:T(8,128)S(1)}, f32[32,256]{1,0:T(8,128)S(1)}, u32[]{:S(2)}, u32[]{:S(2)}) collective-permute-start(f32[32,256]{1,0:T(8,128)S(1)} %convolution_add_fusion.16), channel_id=1, source_target_pairs={{32,0},{40,8},{48,16},{56,24},{64,32},{72,40},{80,48},{88,56},{96,... | collective-permute-start | bytes 98312 | tf_op jit(solution)/shard_map/ppermute | solution.py:24
  317.0 11.7 %collective-permute-start.18 = (f32[256,256]{1,0:T(8,128)S(1)}, f32[256,256]{1,0:T(8,128)S(1)}, u32[]{:S(2)}, u32[]{:S(2)}) collective-permute-start(f32[256,256]{1,0:T(8,128)S(1)} %fusion.60), channel_id=1, source_target_pairs={{32,0},{40,8},{48,16},{56,24},{64,32},{72,40},{80,48},{88,56},{96,... | collective-permute-start | bytes 786440 | tf_op jit(solution)/shard_map/ppermute | solution.py:24
  319.3 12.0 %collective-permute-start.17 = (f32[32,256]{1,0:T(8,128)S(1)}, f32[32,256]{1,0:T(8,128)S(1)}, u32[]{:S(2)}, u32[]{:S(2)}) collective-permute-start(f32[32,256]{1,0:T(8,128)S(1)} %convolution_add_fusion.15), channel_id=1, source_target_pairs={{64,0},{72,8},{80,16},{88,24},{96,32},{104,40},{112,48},{120,56},{... | collective-permute-start | bytes 98312 | tf_op jit(solution)/shard_map/ppermute | solution.py:24
  329.0 11.2 %collective-permute-start.20 = (f32[256,256]{1,0:T(8,128)S(1)}, f32[256,256]{1,0:T(8,128)S(1)}, u32[]{:S(2)}, u32[]{:S(2)}) collective-permute-start(f32[256,256]{1,0:T(8,128)S(1)} %fusion.61), channel_id=1, source_target_pairs={{64,0},{72,8},{80,16},{88,24},{96,32},{104,40},{112,48},{120,56},{... | collective-permute-start | bytes 786440 | tf_op jit(solution)/shard_map/ppermute | solution.py:24
  331.6 11.0 %collective-permute-start.19 = (f32[32,256]{1,0:T(8,128)S(1)}, f32[32,256]{1,0:T(8,128)S(1)}, u32[]{:S(2)}, u32[]{:S(2)}) collective-permute-start(f32[32,256]{1,0:T(8,128)S(1)} %convolution_add_fusion.14), channel_id=1, source_target_pairs={{128,0},{136,8},{144,16},{152,24},{160,32},{168,40},{176,48},{184,... | collective-permute-start | bytes 98312 | tf_op jit(solution)/shard_map/ppermute | solution.py:24
  340.6 17.1 %collective-permute-start.22 = (f32[256,256]{1,0:T(8,128)S(1)}, f32[256,256]{1,0:T(8,128)S(1)}, u32[]{:S(2)}, u32[]{:S(2)}) collective-permute-start(f32[256,256]{1,0:T(8,128)S(1)} %fusion.62), channel_id=1, source_target_pairs={{128,0},{136,8},{144,16},{152,24},{160,32},{168,40},{176,48},{184,... | collective-permute-start | bytes 786440 | tf_op jit(solution)/shard_map/ppermute | solution.py:24
  342.9 15.2 %collective-permute-start.21 = (f32[32,256]{1,0:T(8,128)S(1)}, f32[32,256]{1,0:T(8,128)S(1)}, u32[]{:S(2)}, u32[]{:S(2)}) collective-permute-start(f32[32,256]{1,0:T(8,128)S(1)} %convolution_add_fusion.13), channel_id=1, source_target_pairs={{256,0},{264,8},{272,16},{280,24},{288,32},{296,40},{304,48},{312,... | collective-permute-start | bytes 98312 | tf_op jit(solution)/shard_map/ppermute | solution.py:24
  358.1 0.7 copy-start
  359.2 3.5 collective-permute-start.23
  536.0 8.6 %collective-permute-start.24 = (f32[32,256]{1,0:T(8,128)S(1)}, f32[32,256]{1,0:T(8,128)S(1)}, u32[]{:S(2)}, u32[]{:S(2)}) collective-permute-start(f32[32,256]{1,0:T(8,128)S(1)} %get-tuple-element.574), channel_id=1, source_target_pairs={{0,8},{8,16},{16,24},{24,32},{32,40},{40,48},{48,56},{56,64},{64,7... | collective-permute-start | bytes 98312 | tf_op jit(solution)/shard_map/ppermute | solution.py:24
  544.9 9.1 %collective-permute-start.25 = (f32[32,256]{1,0:T(8,128)S(1)}, f32[32,256]{1,0:T(8,128)S(1)}, u32[]{:S(2)}, u32[]{:S(2)}) collective-permute-start(f32[32,256]{1,0:T(8,128)S(1)} %convolution_add_fusion.11), channel_id=1, source_target_pairs={{0,16},{8,24},{16,32},{24,40},{32,48},{40,56},{48,64},{56,72},{64,... | collective-permute-start | bytes 98312 | tf_op jit(solution)/shard_map/ppermute | solution.py:24
  554.4 120.9 %copy-start.1 = (f32[256,256]{1,0:T(8,128)S(1)}, f32[256,256]{1,0:T(8,128)}, u32[]{:S(2)}) copy-start(f32[256,256]{1,0:T(8,128)} %copy-done) | copy-start | bytes 786436
  554.4 9.6 %collective-permute-start.26 = (f32[32,256]{1,0:T(8,128)S(1)}, f32[32,256]{1,0:T(8,128)S(1)}, u32[]{:S(2)}, u32[]{:S(2)}) collective-permute-start(f32[32,256]{1,0:T(8,128)S(1)} %convolution_add_fusion.10), channel_id=1, source_target_pairs={{0,32},{8,40},{16,48},{24,56},{32,64},{40,72},{48,80},{56,88},{64,... | collective-permute-start | bytes 98312 | tf_op jit(solution)/shard_map/ppermute | solution.py:24
  564.3 7.0 collective-permute-start.27
  571.7 7.9 collective-permute-start.28
  579.9 9.7 %collective-permute-start.29 = (f32[32,256]{1,0:T(8,128)S(1)}, f32[32,256]{1,0:T(8,128)S(1)}, u32[]{:S(2)}, u32[]{:S(2)}) collective-permute-start(f32[32,256]{1,0:T(8,128)S(1)} %convolution_add_fusion.7), channel_id=1, source_target_pairs={{0,256},{8,264},{16,272},{24,280},{32,288},{40,296},{48,304},{56,3... | collective-permute-start | bytes 98312 | tf_op jit(solution)/shard_map/ppermute | solution.py:24
  590.0 8.6 %collective-permute-start.30 = (f32[32,256]{1,0:T(8,128)S(1)}, f32[32,256]{1,0:T(8,128)S(1)}, u32[]{:S(2)}, u32[]{:S(2)}) collective-permute-start(f32[32,256]{1,0:T(8,128)S(1)} %convolution_add_fusion.6), channel_id=1, source_target_pairs={{0,8},{8,16},{16,24},{24,32},{32,40},{40,48},{48,56},{56,64},{64,7... | collective-permute-start | bytes 98312 | tf_op jit(solution)/shard_map/ppermute | solution.py:24
  641.4 3.5 collective-permute-start.31
  645.2 5.8 collective-permute-start.32
  651.4 7.3 collective-permute-start.33
  659.0 6.0 collective-permute-start.34
  665.4 6.7 collective-permute-start.35
  672.4 2.9 collective-permute-start.36
  675.6 17.8 %collective-permute-start.37 = (f32[32,256]{1,0:T(8,128)S(1)}, f32[32,256]{1,0:T(8,128)S(1)}, u32[]{:S(2)}, u32[]{:S(2)}) collective-permute-start(f32[32,256]{1,0:T(8,128)S(1)} %convolution_add_fusion), channel_id=1, source_target_pairs={{8,0},{16,8},{24,16},{32,24},{40,32},{48,40},{56,48},{64,56},{72,6... | collective-permute-start | bytes 98312 | tf_op jit(solution)/shard_map/ppermute | solution.py:24
